TPU v7x, 128 devices: a whole 4x4x4 slice. The times are simulated.
128 devices in a mesh: req: 8 (over x_lo, y), grp: 16 (over z, x_hi, core).
Axes of the slice: x: 4 (x_hi: 2, x_lo: 2; x = x_hi * 2 + x_lo), y: 4, z: 4, core: 2. Of those that a mesh axis runs over, the one named last changes fastest.
Arguments:
- residual: bfloat16 [8, 16, 128, 4096], P('req', 'grp'), may hold values from -64 to 64
- suffix_proj: bfloat16 [8, 16, 3, 128, 4096], P('req', 'grp'), may hold values from -256 to 256
- prefix_cache: bfloat16 [8, 16, 2, 128, 4096], P('req', 'grp'), may hold values from -8 to 8
- owner_req: int32 [16], replicated, may hold values from 0 to 7, as said below
- lengths: int32 [8, 16], P('req', 'grp'), may hold values from 8 to 128, as said below
- norm_gain: float32 [4096], replicated, may hold values from 0.1 to 1.9
- up_weight: bfloat16 [12288, 4096], P('grp'), may hold values from -0.09375 to 0.09375
- down_weight: bfloat16 [12288, 4096], P('grp'), may hold values from -0.0546875 to 0.0546875
Outputs:
- output: bfloat16 [8, 16, 128, 4096], P('req', 'grp')
Inputs may be any that keep to these rules, and one draw needn't show every extreme that they name: owner_req[g] is the req index whose cache block holds group g's prefix. The first lengths[r, g] of the 128 slots of a request are live; in every req index one request fills all 128 slots.
All inputs are finite; a program needn't handle non-finite values.
Results may differ from a plain program's by a relative error of at most 0.014.
Values may be sent and summed in bfloat16 or wider, within the bound.
No kernel may reach another device: no remote copies, remote signals or barrier semaphores. Data moves between devices by JAX's collectives and lax.ppermute only.
A program may use at most 128 MiB of HBM per device.

v0:
```python
import math
import jax
import jax.numpy as jnp
from jax import lax
from jax.sharding import PartitionSpec as P

HEADS = 32
NORM_EPS = 1e-05


def from_root(value, axis, source):
    kept = jnp.where(lax.axis_index(axis) == source, value, 0).astype(value.dtype)
    return lax.psum(kept, axis)


def head_slopes(head_count):
    return jnp.exp2(-8.0 * jnp.arange(1, head_count + 1, dtype=jnp.float32) / head_count)


def attend(queries, key_rows, value_rows, key_pos, query_pos, causal):
    head_size = queries.shape[2]
    scores = jnp.einsum("qhe,khe->hqk", queries, key_rows, preferred_element_type=jnp.float32)
    scores = scores * (1.0 / math.sqrt(head_size))
    offsets = (key_pos[None, :] - query_pos[:, None]).astype(jnp.float32)
    scores = scores + head_slopes(queries.shape[1])[:, None, None] * offsets[None, :, :]
    if causal:
        scores = jnp.where((key_pos[None, :] <= query_pos[:, None])[None], scores, -jnp.inf)
    row_max = jnp.max(scores, axis=2)
    weights = jnp.exp(scores - row_max[:, :, None])
    row_total = jnp.sum(weights, axis=2)
    context = jnp.einsum(
        "hqk,khe->qhe", weights.astype(jnp.bfloat16), value_rows, preferred_element_type=jnp.float32
    )
    return (row_max, row_total, context)


def merge_parts(first, second):
    joint_max = jnp.maximum(first[0], second[0])
    first_scale = jnp.exp(first[0] - joint_max)
    second_scale = jnp.exp(second[0] - joint_max)
    numer = first[2] * first_scale.T[:, :, None] + second[2] * second_scale.T[:, :, None]
    denom = first[1] * first_scale + second[1] * second_scale
    merged = numer / denom.T[:, :, None]
    return merged.reshape(merged.shape[0], merged.shape[1] * merged.shape[2])


def layer_norm(state, norm_gain):
    values = state.astype(jnp.float32)
    center = values - jnp.mean(values, axis=-1, keepdims=True)
    spread = jnp.mean(center * center, axis=-1, keepdims=True)
    return (center * lax.rsqrt(spread + NORM_EPS) * norm_gain).astype(jnp.bfloat16)


def body(
    residual, suffix_proj, prefix_cache, owner_req, lengths, norm_gain, up_weight, down_weight
):
    slot_count = residual.shape[2]
    feature_count = residual.shape[3]
    prefix_count = prefix_cache.shape[3]
    head_count = HEADS
    head_size = feature_count // head_count
    block = suffix_proj[0, 0].reshape(3, slot_count, head_count, head_size)
    query_pos = prefix_count + jnp.arange(slot_count, dtype=jnp.int32)
    prefix_pos = jnp.arange(prefix_count, dtype=jnp.int32)
    group_index = lax.axis_index("grp")
    owner_index = lax.dynamic_index_in_dim(owner_req, group_index, 0, keepdims=False)
    cached = from_root(prefix_cache[0, 0], "req", owner_index)
    cached = cached.reshape(2, prefix_count, head_count, head_size)
    first = attend(block[0], cached[0], cached[1], prefix_pos, query_pos, False)
    second = attend(block[0], block[1], block[2], query_pos, query_pos, True)
    context = merge_parts(first, second)
    states = (residual[0, 0].astype(jnp.float32) + context).astype(jnp.bfloat16)
    normed = layer_norm(states, norm_gain)
    preactivation = lax.dot_general(
        lax.all_gather(normed, "grp", axis=0, tiled=True),
        up_weight,
        (((1,), (1,)), ((), ())),
        preferred_element_type=jnp.float32,
    )
    hidden = jax.nn.gelu(preactivation, approximate=False).astype(jnp.bfloat16)
    partial_term = jnp.dot(hidden, down_weight, preferred_element_type=jnp.float32).astype(
        jnp.bfloat16
    )
    mlp_sum = lax.psum_scatter(
        lax.optimization_barrier(partial_term).astype(jnp.float32).astype(jnp.bfloat16),
        "grp",
        scatter_dimension=0,
        tiled=True,
    ).astype(jnp.float32)
    live = jnp.arange(slot_count, dtype=jnp.int32) < lengths[0, 0]
    combined = states.astype(jnp.float32) + mlp_sum
    output = jnp.where(live[:, None], combined, 0.0).astype(jnp.bfloat16)
    return output[None, None]


def solution(mesh):
    placed = (
        P("req", "grp", None, None),
        P("req", "grp", None, None, None),
        P("req", "grp", None, None, None),
        P(),
        P("req", "grp"),
        P(),
        P("grp", None),
        P("grp", None),
    )
    return jax.shard_map(
        body, mesh=mesh, in_specs=placed, out_specs=P("req", "grp", None, None), check_vma=False
    )
```

profile of v0, /device:TPU:0, one launch (start us, length us, event | category | flops | bytes accessed | tf_op | source)
XLA Modules:
  0.0 429.7 jit_solution(6529954950171514383)
XLA Ops:
  6.5 0.0 all-reduce.2.cloned.1.call-start
  6.5 3.1 copy.16
  9.7 1.2 dynamic_slice.4
  11.6 1.4 select_bitcast_fusion
  13.0 0.0 all-reduce.2.cloned.1.call-update
  13.0 0.0 copy-start.2
  13.1 0.0 all-gather.2.cloned.1.call-start
  13.1 3.5 fusion.96
  16.7 1.6 copy.35
  18.3 2.3 copy.36
  20.6 1.3 copy.25
  21.9 0.0 copy-done.2
  21.9 1.6 copy.28
  23.5 0.1 broadcast_compare_fusion
  23.6 0.1 subtract_convert_fusion
  23.7 3.4 fusion.99
  27.1 70.7 %all-reduce.2.cloned.1.call-done = bf16[2,128,4096]{1,2,0:T(8,128)(2,1)} async-done(((bf16[2,128,4096]{1,2,0:T(8,128)(2,1)}), bf16[2,128,4096]{1,2,0:T(8,128)(2,1)}) %all-reduce.2.cloned.1.call-update) | async-done | bytes 2097168 | tf_op jit(solution)/shard_map/psum | solution.py:13
  97.9 0.0 copy-start.5
  97.9 1.8 fusion.97
  99.7 0.0 copy-start.4
  99.7 0.0 copy-start.6
  99.7 0.7 fusion.98
  100.5 0.5 fusion.56
  100.9 0.0 copy-done.5
  100.9 1.0 fusion.51
  102.0 0.0 copy-done.4
  102.0 0.0 copy-done.6
  102.0 0.0 copy-start.7
  102.0 2.5 convert_reduce_fusion
  104.6 1.9 copy.27
  106.5 0.0 copy-start
  106.5 2.5 fusion.47
  109.1 0.0 copy-done.7
  109.1 1.4 fusion.43
  110.5 0.0 all-gather.2.cloned.1.call-update
  110.5 0.2 reduce-scatter.2.cloned.1.call-start
  110.7 109.1 %all-gather.2.cloned.1.call-done = bf16[2048,4096]{1,0:T(8,128)(2,1)} async-done(((bf16[128,4096]{1,0:T(8,128)(2,1)}), bf16[2048,4096]{1,0:T(8,128)(2,1)}) %all-gather.2.cloned.1.call-update) | async-done | bytes 16777232 | tf_op jit(solution)/shard_map/all_gather | solution.py:75
  219.8 55.8 %convolution_convert_fusion = bf16[2048,4096]{1,0:T(8,128)(2,1)} fusion(bf16[768,4096]{1,0:T(8,128)(2,1)} %param.15, bf16[2048,4096]{1,0:T(8,128)(2,1)} %all-gather.2.cloned.1.call-done, bf16[768,4096]{1,0:T(8,128)(2,1)} %param.14), kind=kOutput, calls=%fused_computation | convolution fusion | flops 25880428544 | bytes 46137344 | tf_op jit(solution)/shard_map/dot_general | solution.py:81
  275.6 0.0 copy-done
  275.6 0.0 copy-start.1
  275.6 0.0 copy-start.3
  275.6 0.0 reduce-scatter.2.cloned.1.call-update
  276.5 144.0 %reduce-scatter.2.cloned.1.call-done = bf16[128,4096]{1,0:T(8,128)(2,1)} async-done(((bf16[2048,4096]{1,0:T(8,128)(2,1)}), bf16[128,4096]{1,0:T(8,128)(2,1)}) %reduce-scatter.2.cloned.1.call-update) | async-done | bytes 1048592 | tf_op jit(solution)/shard_map/reduce_scatter | solution.py:84
  420.5 0.0 copy-done.1
  420.5 0.0 copy-done.3
  420.5 2.6 fusion.58
  (6 shorter events, 0.1 us)
Async XLA Ops:
  6.5 91.3 %all-reduce.2.cloned.1.call-start = ((), (), s32[]{:S(2)}) async-start(), calls=%async_computation.1 | async-start | bytes 4194304 | tf_op jit(solution)/shard_map/psum | solution.py:13
  13.0 8.8 %copy-start.2 = (bf16[1,1,128,4096]{3,2,1,0:T(8,128)(2,1)S(1)}, bf16[1,1,128,4096]{3,2,1,0:T(8,128)(2,1)}, u32[]{:S(2)}) copy-start(bf16[1,1,128,4096]{3,2,1,0:T(8,128)(2,1)} %param.8) | copy-start | bytes 3145732
  13.1 206.8 %all-gather.2.cloned.1.call-start = ((), (), s32[]{:S(2)}) async-start(), calls=%async_computation.2 | async-start | bytes 17825792 | tf_op jit(solution)/shard_map/all_gather | solution.py:75
  97.9 3.1 copy-start.5
  99.7 2.3 copy-start.4
  99.7 2.3 copy-start.6
  102.0 7.0 %copy-start.7 = (f32[4096]{0:T(1024)S(1)}, f32[4096]{0:T(1024)}, u32[]{:S(2)}) copy-start(f32[4096]{0:T(1024)} %param.13) | copy-start | bytes 49156
  106.5 169.2 %copy-start = (f32[128,4096]{1,0:T(8,128)}, f32[128,4096]{1,0:T(8,128)S(1)}, u32[]{:S(2)}) copy-start(f32[128,4096]{1,0:T(8,128)S(1)} %copy.27) | copy-start | bytes 6291460
  110.5 310.0 %reduce-scatter.2.cloned.1.call-start = ((), (), s32[]{:S(2)}) async-start(), calls=%async_computation.3 | async-start | bytes 17825792 | tf_op jit(solution)/shard_map/reduce_scatter | solution.py:84
  275.6 144.9 %copy-start.1 = (f32[128,4096]{1,0:T(8,128)S(1)}, f32[128,4096]{1,0:T(8,128)}, u32[]{:S(2)}) copy-start(f32[128,4096]{1,0:T(8,128)} %copy-done) | copy-start | bytes 6291460
  275.6 144.9 %copy-start.3 = (bf16[1,1,128,4096]{3,2,1,0:T(8,128)(2,1)S(1)}, bf16[1,1,128,4096]{3,2,1,0:T(8,128)(2,1)}, u32[]{:S(2)}) copy-start(bf16[1,1,128,4096]{3,2,1,0:T(8,128)(2,1)} %param.8) | copy-start | bytes 3145732
Sparse Core Ops, SparseCore 0:
  13.2 84.6 all-reduce.1
  110.6 109.1 all-gather.1
  275.8 144.6 reduce-scatter.1
where the time goes:
time: 430 us
  waiting for transfers between devices  324 us (75%)
  matrix products  63 us (15%)
  local copies, waits for them, and re-layouts  18.5 us (4%)
  between operations  14.7 us (3%)
  other arithmetic  9.27 us (2%)
    reduce_scatter x1, waiting for transfers between devices, body(): lax.psum_scatter(lax.optimization_barrier(partial_term).astype(jnp.float3...  144 us
    all_gather x1, waiting for transfers between devices, body(): lax.all_gather(normed, 'grp', axis=0, tiled=True)  109 us
    psum x1, waiting for transfers between devices, from_root(): return lax.psum(kept, axis)  70.7 us
    dot_general x1, matrix products, body(): jnp.dot(hidden, down_weight, preferred_element_type=jnp.float32)  55.8 us
  transfers between devices with their start and end apart: 3, of which 3 were waited for; matrix products, arithmetic and copies ran while one was open for 3% of the time, Pallas kernels for 0%

commit v1 on v0

--- a/solution.py
+++ b/solution.py
@@ -72,7 +72,9 @@
     states = (residual[0, 0].astype(jnp.float32) + context).astype(jnp.bfloat16)
     normed = layer_norm(states, norm_gain)
     preactivation = lax.dot_general(
-        lax.all_gather(normed, "grp", axis=0, tiled=True),
+        jnp.concatenate(
+            lax.all_to_all(jnp.stack([normed] * lax.axis_size("grp")), "grp", 0, 0), axis=0
+        ),
         up_weight,
         (((1,), (1,)), ((), ())),
         preferred_element_type=jnp.float32,

time: 430 us -> 515 us (1.20)
  blocking collectives: 0 us -> 193 us
  waiting for transfers between devices: 324 us -> 215 us
    all_to_all x0 -> x1, blocking collectives: none -> 193 us  [body(): lax.all_to_all(jnp.stack([normed] * lax.axis_size('grp')), 'grp', 0, 0)]
    all_gather x1 -> x0, waiting for transfers between devices: 109 us -> none  [body(): lax.all_gather(normed, 'grp', axis=0, tiled=True)]
  transfers between devices with their start and end apart: 3 -> 2, of which waited for: 3 -> 2; matrix products, arithmetic and copies ran while one was open for 3% -> 3% of each run, Pallas kernels for 0% -> 0%
where the time goes in v1:
time: 515 us
  waiting for transfers between devices  215 us (42%)
  blocking collectives  193 us (37%)
  matrix products  63 us (12%)
  local copies, waits for them, and re-layouts  20.6 us (4%)
  between operations  15 us (3%)
  other arithmetic  8.29 us (2%)
    all_to_all x1, blocking collectives, body(): lax.all_to_all(jnp.stack([normed] * lax.axis_size('grp')), 'grp', 0, 0)  193 us
    reduce_scatter x1, waiting for transfers between devices, body(): lax.psum_scatter(lax.optimization_barrier(partial_term).astype(jnp.float3...  144 us
    psum x1, waiting for transfers between devices, from_root(): return lax.psum(kept, axis)  70.7 us
    dot_general x1, matrix products, body(): jnp.dot(hidden, down_weight, preferred_element_type=jnp.float32)  55.8 us
  transfers between devices with their start and end apart: 2, of which 2 were waited for; matrix products, arithmetic and copies ran while one was open for 3% of the time, Pallas kernels for 0%

profile of v1, /device:TPU:0, one launch (start us, length us, event | category | flops | bytes accessed | tf_op | source)
XLA Modules:
  0.0 514.6 jit_solution(12218217411491372346)
XLA Ops:
  6.5 0.0 all-reduce.2.cloned.1.call-start
  6.5 3.1 copy.16
  9.7 1.2 dynamic_slice.4
  11.6 1.4 select_bitcast_fusion
  13.0 0.0 all-reduce.2.cloned.1.call-update
  13.0 0.0 copy-start.2
  13.0 0.0 reduce-scatter.2.cloned.1.call-start
  13.1 3.6 fusion.96
  16.7 1.6 copy.35
  18.3 2.3 copy.36
  20.6 1.3 copy.25
  21.9 0.0 copy-done.2
  21.9 1.6 copy.28
  23.6 0.1 broadcast_compare_fusion
  23.6 0.1 subtract_convert_fusion
  23.7 3.4 fusion.99
  27.2 70.7 %all-reduce.2.cloned.1.call-done = bf16[2,128,4096]{1,2,0:T(8,128)(2,1)} async-done(((bf16[2,128,4096]{1,2,0:T(8,128)(2,1)}), bf16[2,128,4096]{1,2,0:T(8,128)(2,1)}) %all-reduce.2.cloned.1.call-update) | async-done | bytes 2097168 | tf_op jit(solution)/shard_map/psum | solution.py:13
  97.9 0.0 copy-start.5
  97.9 1.8 fusion.97
  99.7 0.0 copy-start.4
  99.7 0.0 copy-start.6
  99.7 0.7 fusion.98
  100.5 0.5 fusion.56
  100.9 0.0 copy-done.5
  100.9 1.0 fusion.51
  102.0 0.0 copy-done.4
  102.0 0.0 copy-done.6
  102.0 0.0 copy-start.7
  102.0 2.5 convert_reduce_fusion
  104.6 1.9 copy.27
  106.5 0.0 copy-start
  106.5 2.5 fusion.47
  109.1 0.0 copy-done.7
  109.1 0.4 fusion.43
  109.5 2.0 stack.2
  111.5 0.0 copy-done
  111.5 193.0 %all_to_all.5 = bf16[16,128,4096]{2,1,0:T(8,128)(2,1)} all-to-all(bf16[16,128,4096]{2,1,0:T(8,128)(2,1)S(1)} %stack.2), channel_id=1, replica_groups=mesh['req'=8,'grp'=16] {'grp'}, dimensions={0} | all-to-all | bytes 33554432 | tf_op jit(solution)/shard_map/all_to_all | solution.py:76
  304.5 55.8 %convolution_convert_fusion = bf16[2048,4096]{1,0:T(8,128)(2,1)} fusion(bf16[768,4096]{1,0:T(8,128)(2,1)} %param.15, bf16[2048,4096]{1,0:T(8,128)(2,1)} %bitcast.62, bf16[768,4096]{1,0:T(8,128)(2,1)} %param.14), kind=kOutput, calls=%fused_computation | convolution fusion | flops 25880428544 | bytes 46137344 | tf_op jit(solution)/shard_map/dot_general | solution.py:83
  360.3 0.0 copy-start.1
  360.4 0.0 copy-start.3
  360.4 0.0 reduce-scatter.2.cloned.1.call-update
  361.2 143.9 %reduce-scatter.2.cloned.1.call-done = bf16[128,4096]{1,0:T(8,128)(2,1)} async-done(((bf16[2048,4096]{1,0:T(8,128)(2,1)}), bf16[128,4096]{1,0:T(8,128)(2,1)}) %reduce-scatter.2.cloned.1.call-update) | async-done | bytes 1048592 | tf_op jit(solution)/shard_map/reduce_scatter | solution.py:86
  505.1 0.0 copy-done.1
  505.1 0.0 copy-done.3
  505.1 2.6 fusion.58
  (6 shorter events, 0.1 us)
Async XLA Ops:
  6.5 91.3 %all-reduce.2.cloned.1.call-start = ((), (), s32[]{:S(2)}) async-start(), calls=%async_computation.2 | async-start | bytes 4194304 | tf_op jit(solution)/shard_map/psum | solution.py:13
  13.0 8.9 %copy-start.2 = (bf16[1,1,128,4096]{3,2,1,0:T(8,128)(2,1)S(1)}, bf16[1,1,128,4096]{3,2,1,0:T(8,128)(2,1)}, u32[]{:S(2)}) copy-start(bf16[1,1,128,4096]{3,2,1,0:T(8,128)(2,1)} %param.8) | copy-start | bytes 3145732
  13.0 492.1 %reduce-scatter.2.cloned.1.call-start = ((), (), s32[]{:S(2)}) async-start(), calls=%async_computation.3 | async-start | bytes 17825792 | tf_op jit(solution)/shard_map/reduce_scatter | solution.py:86
  97.9 3.1 copy-start.5
  99.7 2.3 copy-start.4
  99.7 2.3 copy-start.6
  102.0 7.0 %copy-start.7 = (f32[4096]{0:T(1024)S(1)}, f32[4096]{0:T(1024)}, u32[]{:S(2)}) copy-start(f32[4096]{0:T(1024)} %param.13) | copy-start | bytes 49156
  106.5 5.0 copy-start
  360.3 144.8 %copy-start.1 = (f32[128,4096]{1,0:T(8,128)S(1)}, f32[128,4096]{1,0:T(8,128)}, u32[]{:S(2)}) copy-start(f32[128,4096]{1,0:T(8,128)} %copy-done) | copy-start | bytes 6291460
  360.4 144.8 %copy-start.3 = (bf16[1,1,128,4096]{3,2,1,0:T(8,128)(2,1)S(1)}, bf16[1,1,128,4096]{3,2,1,0:T(8,128)(2,1)}, u32[]{:S(2)}) copy-start(bf16[1,1,128,4096]{3,2,1,0:T(8,128)(2,1)} %param.8) | copy-start | bytes 3145732
Sparse Core Ops, SparseCore 0:
  13.2 84.6 all-reduce.1
  360.5 144.5 reduce-scatter.1

commit v2 on v0

--- a/solution.py
+++ b/solution.py
@@ -10,7 +10,7 @@
 
 def from_root(value, axis, source):
     kept = jnp.where(lax.axis_index(axis) == source, value, 0).astype(value.dtype)
-    return lax.psum(kept, axis)
+    return jnp.sum(lax.all_gather(kept, axis), axis=0)
 
 
 def head_slopes(head_count):

time: 430 us -> 528 us (1.23)
  waiting for transfers between devices: 324 us -> 411 us
  other arithmetic: 9.27 us -> 18.5 us
    all_gather x0 -> x1, waiting for transfers between devices: none -> 160 us  [from_root(): return jnp.sum(lax.all_gather(kept, axis), axis=0)]
    psum x1 -> x0, waiting for transfers between devices: 70.7 us -> none  [from_root(): return lax.psum(kept, axis)]
    reduce_sum x0 -> x1, other arithmetic: none -> 9.18 us  [from_root(): return jnp.sum(lax.all_gather(kept, axis), axis=0)]
where the time goes in v2:
time: 528 us
  waiting for transfers between devices  411 us (78%)
  matrix products  64.2 us (12%)
  local copies, waits for them, and re-layouts  18.7 us (4%)
  other arithmetic  18.5 us (4%)
  between operations  14.7 us (3%)
    all_gather x1, waiting for transfers between devices, from_root(): return jnp.sum(lax.all_gather(kept, axis), axis=0)  160 us
    reduce_scatter x1, waiting for transfers between devices, body(): lax.psum_scatter(lax.optimization_barrier(partial_term).astype(jnp.float3...  144 us
    all_gather x1, waiting for transfers between devices, body(): lax.all_gather(normed, 'grp', axis=0, tiled=True)  108 us
    dot_general x1, matrix products, body(): jnp.dot(hidden, down_weight, preferred_element_type=jnp.float32)  55.8 us
  transfers between devices with their start and end apart: 3, of which 3 were waited for; matrix products, arithmetic and copies ran while one was open for 3% of the time, Pallas kernels for 0%

profile of v2, /device:TPU:0, one launch (start us, length us, event | category | flops | bytes accessed | tf_op | source)
XLA Modules:
  0.0 527.7 jit_solution(11478366809439364006)
XLA Ops:
  6.5 0.0 all-gather.6.cloned.1.call-start
  6.5 1.2 dynamic_slice.4
  8.4 1.5 broadcast_select_fusion
  9.9 0.0 all-gather.6.cloned.1.call-update
  9.9 0.0 copy-start.2
  9.9 0.0 all-gather.4.cloned.1.call-start
  10.0 3.6 fusion.96
  13.6 1.6 copy.47
  15.2 0.0 copy-start.4
  15.2 2.7 copy.48
  17.9 1.3 copy.37
  19.2 0.0 copy-done.2
  19.2 1.6 copy.40
  20.8 0.1 broadcast_compare_fusion
  20.9 0.1 subtract_convert_fusion
  21.0 3.3 fusion.99
  24.3 0.0 copy-done.4
  24.3 159.9 %all-gather.6.cloned.1.call-done = bf16[8,1,2,128,4096]{4,3,2,1,0:T(8,128)(2,1)} async-done(((bf16[1,1,2,128,4096]{4,3,2,1,0:T(8,128)(2,1)}), bf16[8,1,2,128,4096]{4,3,2,1,0:T(8,128)(2,1)}) %all-gather.6.cloned.1.call-update) | async-done | bytes 16777232 | tf_op jit(solution)/shard_map/all_gather | solution.py:13
  184.2 9.2 %reduce_sum.52 = bf16[2,128,4096]{2,1,0:T(8,128)(2,1)S(1)} reduce(bf16[8,1,2,128,4096]{4,3,2,1,0:T(8,128)(2,1)} %all-gather.6.cloned.1.call-done, bf16[]{:T(256)} %constant.13.clone.1), dimensions={0,1}, to_apply=%region_0.1 | reduce | flops 7340032 | bytes 18874370 | tf_op jit(solution)/shard_map/reduce_sum | solution.py:13
  193.4 1.5 fusion.97
  194.9 1.6 copy.28
  196.5 1.6 copy.27
  198.1 0.0 copy-start.6
  198.1 0.0 copy-start.5
  198.1 0.0 copy-start.7
  198.2 2.1 fusion.98
  200.2 0.5 fusion.56
  200.7 0.0 copy-done.6
  200.7 1.0 fusion.51
  201.8 0.0 copy-done.5
  201.8 0.0 copy-done.7
  201.8 0.0 copy-start.8
  201.8 2.5 convert_reduce_fusion
  204.4 1.9 copy.39
  206.3 0.0 copy-start
  206.3 2.5 fusion.47
  208.9 0.0 copy-done.8
  208.9 1.4 fusion.43
  210.3 0.0 all-gather.4.cloned.1.call-update
  210.3 0.2 reduce-scatter.2.cloned.1.call-start
  210.5 107.6 %all-gather.4.cloned.1.call-done = bf16[2048,4096]{1,0:T(8,128)(2,1)} async-done(((bf16[128,4096]{1,0:T(8,128)(2,1)}), bf16[2048,4096]{1,0:T(8,128)(2,1)}) %all-gather.4.cloned.1.call-update) | async-done | bytes 16777232 | tf_op jit(solution)/shard_map/all_gather | solution.py:75
  318.1 55.8 %convolution_convert_fusion = bf16[2048,4096]{1,0:T(8,128)(2,1)} fusion(bf16[768,4096]{1,0:T(8,128)(2,1)} %param.15, bf16[2048,4096]{1,0:T(8,128)(2,1)} %all-gather.4.cloned.1.call-done, bf16[768,4096]{1,0:T(8,128)(2,1)} %param.14), kind=kOutput, calls=%fused_computation | convolution fusion | flops 25880428544 | bytes 46137344 | tf_op jit(solution)/shard_map/dot_general | solution.py:81
  373.9 0.0 copy-done
  373.9 0.0 copy-start.1
  373.9 0.0 copy-start.3
  373.9 0.0 reduce-scatter.2.cloned.1.call-update
  374.8 143.7 %reduce-scatter.2.cloned.1.call-done = bf16[128,4096]{1,0:T(8,128)(2,1)} async-done(((bf16[2048,4096]{1,0:T(8,128)(2,1)}), bf16[128,4096]{1,0:T(8,128)(2,1)}) %reduce-scatter.2.cloned.1.call-update) | async-done | bytes 1048592 | tf_op jit(solution)/shard_map/reduce_scatter | solution.py:84
  518.5 0.0 copy-done.1
  518.5 0.0 copy-done.3
  518.5 2.6 fusion.58
  (6 shorter events, 0.1 us)
Async XLA Ops:
  6.5 177.7 %all-gather.6.cloned.1.call-start = ((), (), s32[]{:S(2)}) async-start(), calls=%async_computation.3 | async-start | bytes 18874368 | tf_op jit(solution)/shard_map/all_gather | solution.py:13
  9.9 9.3 %copy-start.2 = (bf16[1,1,128,4096]{3,2,1,0:T(8,128)(2,1)S(1)}, bf16[1,1,128,4096]{3,2,1,0:T(8,128)(2,1)}, u32[]{:S(2)}) copy-start(bf16[1,1,128,4096]{3,2,1,0:T(8,128)(2,1)} %param.8) | copy-start | bytes 3145732
  9.9 308.2 %all-gather.4.cloned.1.call-start = ((), (), s32[]{:S(2)}) async-start(), calls=%async_computation.1 | async-start | bytes 17825792 | tf_op jit(solution)/shard_map/all_gather | solution.py:75
  15.2 9.1 %copy-start.4 = (bf16[1,1,1,128,4096]{3,4,2,1,0:T(8,128)(2,1)}, bf16[1,1,1,128,4096]{3,4,2,1,0:T(8,128)(2,1)S(1)}, u32[]{:S(2)}) copy-start(bf16[1,1,1,128,4096]{3,4,2,1,0:T(8,128)(2,1)S(1)} %copy.47) | copy-start | bytes 3145732
  198.1 2.6 copy-start.6
  198.1 3.7 copy-start.5
  198.1 3.7 copy-start.7
  201.8 7.0 %copy-start.8 = (f32[4096]{0:T(1024)S(1)}, f32[4096]{0:T(1024)}, u32[]{:S(2)}) copy-start(f32[4096]{0:T(1024)} %param.13) | copy-start | bytes 49156
  206.3 167.6 %copy-start = (f32[128,4096]{1,0:T(8,128)}, f32[128,4096]{1,0:T(8,128)S(1)}, u32[]{:S(2)}) copy-start(f32[128,4096]{1,0:T(8,128)S(1)} %copy.39) | copy-start | bytes 6291460
  210.3 308.2 %reduce-scatter.2.cloned.1.call-start = ((), (), s32[]{:S(2)}) async-start(), calls=%async_computation.2 | async-start | bytes 17825792 | tf_op jit(solution)/shard_map/reduce_scatter | solution.py:84
  373.9 144.6 %copy-start.1 = (f32[128,4096]{1,0:T(8,128)S(1)}, f32[128,4096]{1,0:T(8,128)}, u32[]{:S(2)}) copy-start(f32[128,4096]{1,0:T(8,128)} %copy-done) | copy-start | bytes 6291460
  373.9 144.6 %copy-start.3 = (bf16[1,1,128,4096]{3,2,1,0:T(8,128)(2,1)S(1)}, bf16[1,1,128,4096]{3,2,1,0:T(8,128)(2,1)}, u32[]{:S(2)}) copy-start(bf16[1,1,128,4096]{3,2,1,0:T(8,128)(2,1)} %param.8) | copy-start | bytes 3145732
Sparse Core Ops, SparseCore 0:
  10.1 174.1 all-gather.5
  210.4 107.6 all-gather.3
  374.1 144.3 reduce-scatter.1
